TPU v7x, 512 devices: a whole 4x8x8 slice. The times are simulated.
512 devices in a mesh: team: 16 (over y, core), tm: 32 (over x, z).
Axes of the slice: x: 4, y: 8, z: 8, core: 2. Of those that a mesh axis runs over, the one named last changes fastest.
Arguments:
- transitions: float32 [16, 32, 512, 512], P('team', 'tm'), may hold values from -0.25 to 1.25
- states: float32 [16, 32, 64, 512], P('team', 'tm'), may hold values from -1 to 1
- cotangent: float32 [16, 32, 64, 512], P('team', 'tm'), may hold values from -2.4 to 2.4
- terminal: float32 [16, 64, 512], P('team'), may hold values from -6 to 6
- incidence: int32 [16, 32, 32, 2048], P('team', 'tm'), may hold values 0 or 1
- measured: float32 [16, 32, 64, 32], P('team', 'tm'), may hold values from -0.12 to 0.12
- obs_gain: float32 [16, 512], P('team'), may hold values from -6 to 6
Outputs:
- adjoint: float32 [16, 32, 64, 512], P('team', 'tm')
- grad_transitions: bfloat16 [16, 32, 512, 512], P('team', 'tm')
All inputs are finite; a program needn't handle non-finite values. No bound on the sum of `incidence` on one device may be relied on, other than what follows from the above.
Results may differ from a plain program's by a relative error of at most 0.001.
Values sent between devices are 32-bit elements; how exact they have to be, the bound alone decides.
No kernel may reach another device: no remote copies, remote signals or barrier semaphores. Data moves between devices by JAX's collectives and lax.ppermute only.
A program may use at most 64 MiB of HBM per device.

v0:
```python
import jax
import jax.numpy as jnp
from jax import lax
from jax.sharding import PartitionSpec as P

STATES = 16
TEAM_STATES = 512
COLS = 64
HIGHEST = lax.Precision.HIGHEST


def from_behind(block, axis, distance):
    devices = range(lax.axis_size(axis))
    route = [(i - distance, i) for i in devices if i - distance in devices]
    return lax.ppermute(block, axis, route)


def matmul(left, right):
    return jnp.dot(left, right, precision=HIGHEST)


def shards(transitions, states, cotangent, terminal, incidence, measured, obs_gain):
    step_count = transitions.shape[1]
    matrices = transitions[0]
    incident = incidence[0].astype(jnp.float32)
    partial_value = jnp.einsum("scr,srl->scl", measured[0], incident, precision=HIGHEST)
    landmark = lax.psum(partial_value, "team")
    injection = jnp.einsum("scl,srl->scr", landmark, incident, precision=HIGHEST)
    driven = cotangent[0] + jnp.repeat(injection, STATES, axis=2) * obs_gain[0][None, None, :]
    offset = jnp.zeros((COLS, TEAM_STATES), jnp.float32)
    moment = 0
    offset = matmul(offset, matrices[moment]) + driven[moment]
    is_last = lax.axis_index("tm") == lax.axis_size("tm") - 1
    start_cot = jnp.where(is_last, terminal[0], jnp.zeros_like(terminal[0]))

    def advance_steps(turn, carried):
        outgoing = carried
        outgoing = matmul(outgoing, matrices[0])
        outgoing = outgoing + offset
        return from_behind(outgoing, "tm", -1) + start_cot

    incoming = lax.fori_loop(0, lax.axis_size("tm") - 1, advance_steps, start_cot)
    running = incoming
    adjoint_list = [None] * step_count
    grad_list = [None] * step_count
    moment = 0
    grad_now = jnp.einsum("cn,cm->nm", running, states[0, moment], precision=HIGHEST)
    grad_list[moment] = grad_now.astype(jnp.bfloat16)
    running = matmul(running, matrices[moment]) + driven[moment]
    adjoint_list[moment] = running
    adjoint = jnp.stack(adjoint_list)[None]
    grad_transitions = jnp.stack(grad_list)[None]
    return (adjoint, grad_transitions)


def solution(mesh):
    placed = (
        P("team", "tm", None, None),
        P("team", "tm", None, None),
        P("team", "tm", None, None),
        P("team", None, None),
        P("team", "tm", None, None),
        P("team", "tm", None, None),
        P("team", None),
    )
    return jax.shard_map(
        shards,
        mesh=mesh,
        in_specs=placed,
        out_specs=(P("team", "tm", None, None), P("team", "tm", None, None)),
        check_vma=False,
    )
```

profile of v0, /device:TPU:30, one launch (start us, length us, event | category | flops | bytes accessed | tf_op | source)
XLA Modules:
  0.0 454.6 jit_solution(4725242785528667431)
XLA Ops:
  10.6 120.1 %all-reduce.2.cloned.1.call-done = f32[64,2048]{1,0:T(8,128)} async-done(((f32[64,2048]{1,0:T(8,128)}), f32[64,2048]{1,0:T(8,128)}) %all-reduce.2.cloned.1.call-update) | async-done | bytes 524304 | tf_op jit(solution)/shard_map/psum | solution.py:27
  134.0 310.5 %while.10 = (s32[]{:T(128)}, f32[64,512]{1,0:T(8,128)S(1)}, f32[1,1,512,512]{3,2,1,0:T(8,128)S(1)}, f32[64,512]{1,0:T(8,128)S(1)}, f32[64,512]{1,0:T(8,128)S(1)}, /*index=5*/s32[]{:T(128)}) while((s32[]{:T(128)}, f32[64,512]{1,0:T(8,128)S(1)}, f32[1,1,512,512]{3,2,1,0:T(8,128)S(1)}, f32[64,512]{1,0:T(8,128)S(1)}, f32[64,512]{1,0:T(8,128)S(1)}, ...), condition=%wide.region_2.3_spmd, body=%wide.region_1.2_spmd.sunk | while | flops 201392128 | bytes 2359405 | solution.py:42
  134.8 6.1 %collective-permute-start = (f32[64,512]{1,0:T(8,128)S(1)}, f32[64,512]{1,0:T(8,128)S(1)}, u32[]{:S(2)}, u32[]{:S(2)}) collective-permute-start(f32[64,512]{1,0:T(8,128)S(1)} %convolution_add_fusion.4), channel_id=1, source_target_pairs={{1,0},{2,1},{3,2},{4,3},{5,4},{6,5},{7,6},{8,7},{9,8},{10,9},{11,1... | collective-permute-start | bytes 393224 | tf_op jit(solution)/shard_map/while/body/eval_jaxpr/ppermute | solution.py:15
  140.9 3.8 collective-permute-done
  145.5 6.5 %collective-permute-start = (f32[64,512]{1,0:T(8,128)S(1)}, f32[64,512]{1,0:T(8,128)S(1)}, u32[]{:S(2)}, u32[]{:S(2)}) collective-permute-start(f32[64,512]{1,0:T(8,128)S(1)} %convolution_add_fusion.4), channel_id=1, source_target_pairs={{1,0},{2,1},{3,2},{4,3},{5,4},{6,5},{7,6},{8,7},{9,8},{10,9},{11,1... | collective-permute-start | bytes 393224 | tf_op jit(solution)/shard_map/while/body/eval_jaxpr/ppermute | solution.py:15
  152.0 3.0 collective-permute-done
  155.8 6.5 %collective-permute-start = (f32[64,512]{1,0:T(8,128)S(1)}, f32[64,512]{1,0:T(8,128)S(1)}, u32[]{:S(2)}, u32[]{:S(2)}) collective-permute-start(f32[64,512]{1,0:T(8,128)S(1)} %convolution_add_fusion.4), channel_id=1, source_target_pairs={{1,0},{2,1},{3,2},{4,3},{5,4},{6,5},{7,6},{8,7},{9,8},{10,9},{11,1... | collective-permute-start | bytes 393224 | tf_op jit(solution)/shard_map/while/body/eval_jaxpr/ppermute | solution.py:15
  162.3 2.5 collective-permute-done
  165.6 6.5 %collective-permute-start = (f32[64,512]{1,0:T(8,128)S(1)}, f32[64,512]{1,0:T(8,128)S(1)}, u32[]{:S(2)}, u32[]{:S(2)}) collective-permute-start(f32[64,512]{1,0:T(8,128)S(1)} %convolution_add_fusion.4), channel_id=1, source_target_pairs={{1,0},{2,1},{3,2},{4,3},{5,4},{6,5},{7,6},{8,7},{9,8},{10,9},{11,1... | collective-permute-start | bytes 393224 | tf_op jit(solution)/shard_map/while/body/eval_jaxpr/ppermute | solution.py:15
  175.3 6.5 %collective-permute-start = (f32[64,512]{1,0:T(8,128)S(1)}, f32[64,512]{1,0:T(8,128)S(1)}, u32[]{:S(2)}, u32[]{:S(2)}) collective-permute-start(f32[64,512]{1,0:T(8,128)S(1)} %convolution_add_fusion.4), channel_id=1, source_target_pairs={{1,0},{2,1},{3,2},{4,3},{5,4},{6,5},{7,6},{8,7},{9,8},{10,9},{11,1... | collective-permute-start | bytes 393224 | tf_op jit(solution)/shard_map/while/body/eval_jaxpr/ppermute | solution.py:15
  181.8 2.5 collective-permute-done
  185.1 6.5 %collective-permute-start = (f32[64,512]{1,0:T(8,128)S(1)}, f32[64,512]{1,0:T(8,128)S(1)}, u32[]{:S(2)}, u32[]{:S(2)}) collective-permute-start(f32[64,512]{1,0:T(8,128)S(1)} %convolution_add_fusion.4), channel_id=1, source_target_pairs={{1,0},{2,1},{3,2},{4,3},{5,4},{6,5},{7,6},{8,7},{9,8},{10,9},{11,1... | collective-permute-start | bytes 393224 | tf_op jit(solution)/shard_map/while/body/eval_jaxpr/ppermute | solution.py:15
  194.8 6.5 %collective-permute-start = (f32[64,512]{1,0:T(8,128)S(1)}, f32[64,512]{1,0:T(8,128)S(1)}, u32[]{:S(2)}, u32[]{:S(2)}) collective-permute-start(f32[64,512]{1,0:T(8,128)S(1)} %convolution_add_fusion.4), channel_id=1, source_target_pairs={{1,0},{2,1},{3,2},{4,3},{5,4},{6,5},{7,6},{8,7},{9,8},{10,9},{11,1... | collective-permute-start | bytes 393224 | tf_op jit(solution)/shard_map/while/body/eval_jaxpr/ppermute | solution.py:15
  204.6 6.5 %collective-permute-start = (f32[64,512]{1,0:T(8,128)S(1)}, f32[64,512]{1,0:T(8,128)S(1)}, u32[]{:S(2)}, u32[]{:S(2)}) collective-permute-start(f32[64,512]{1,0:T(8,128)S(1)} %convolution_add_fusion.4), channel_id=1, source_target_pairs={{1,0},{2,1},{3,2},{4,3},{5,4},{6,5},{7,6},{8,7},{9,8},{10,9},{11,1... | collective-permute-start | bytes 393224 | tf_op jit(solution)/shard_map/while/body/eval_jaxpr/ppermute | solution.py:15
  211.1 2.8 collective-permute-done
  214.6 6.5 %collective-permute-start = (f32[64,512]{1,0:T(8,128)S(1)}, f32[64,512]{1,0:T(8,128)S(1)}, u32[]{:S(2)}, u32[]{:S(2)}) collective-permute-start(f32[64,512]{1,0:T(8,128)S(1)} %convolution_add_fusion.4), channel_id=1, source_target_pairs={{1,0},{2,1},{3,2},{4,3},{5,4},{6,5},{7,6},{8,7},{9,8},{10,9},{11,1... | collective-permute-start | bytes 393224 | tf_op jit(solution)/shard_map/while/body/eval_jaxpr/ppermute | solution.py:15
  221.1 3.8 collective-permute-done
  225.8 6.5 %collective-permute-start = (f32[64,512]{1,0:T(8,128)S(1)}, f32[64,512]{1,0:T(8,128)S(1)}, u32[]{:S(2)}, u32[]{:S(2)}) collective-permute-start(f32[64,512]{1,0:T(8,128)S(1)} %convolution_add_fusion.4), channel_id=1, source_target_pairs={{1,0},{2,1},{3,2},{4,3},{5,4},{6,5},{7,6},{8,7},{9,8},{10,9},{11,1... | collective-permute-start | bytes 393224 | tf_op jit(solution)/shard_map/while/body/eval_jaxpr/ppermute | solution.py:15
  232.2 3.0 collective-permute-done
  236.0 6.5 %collective-permute-start = (f32[64,512]{1,0:T(8,128)S(1)}, f32[64,512]{1,0:T(8,128)S(1)}, u32[]{:S(2)}, u32[]{:S(2)}) collective-permute-start(f32[64,512]{1,0:T(8,128)S(1)} %convolution_add_fusion.4), channel_id=1, source_target_pairs={{1,0},{2,1},{3,2},{4,3},{5,4},{6,5},{7,6},{8,7},{9,8},{10,9},{11,1... | collective-permute-start | bytes 393224 | tf_op jit(solution)/shard_map/while/body/eval_jaxpr/ppermute | solution.py:15
  242.5 2.5 collective-permute-done
  245.8 6.5 %collective-permute-start = (f32[64,512]{1,0:T(8,128)S(1)}, f32[64,512]{1,0:T(8,128)S(1)}, u32[]{:S(2)}, u32[]{:S(2)}) collective-permute-start(f32[64,512]{1,0:T(8,128)S(1)} %convolution_add_fusion.4), channel_id=1, source_target_pairs={{1,0},{2,1},{3,2},{4,3},{5,4},{6,5},{7,6},{8,7},{9,8},{10,9},{11,1... | collective-permute-start | bytes 393224 | tf_op jit(solution)/shard_map/while/body/eval_jaxpr/ppermute | solution.py:15
  252.2 2.5 collective-permute-done
  255.5 6.5 %collective-permute-start = (f32[64,512]{1,0:T(8,128)S(1)}, f32[64,512]{1,0:T(8,128)S(1)}, u32[]{:S(2)}, u32[]{:S(2)}) collective-permute-start(f32[64,512]{1,0:T(8,128)S(1)} %convolution_add_fusion.4), channel_id=1, source_target_pairs={{1,0},{2,1},{3,2},{4,3},{5,4},{6,5},{7,6},{8,7},{9,8},{10,9},{11,1... | collective-permute-start | bytes 393224 | tf_op jit(solution)/shard_map/while/body/eval_jaxpr/ppermute | solution.py:15
  265.3 6.5 %collective-permute-start = (f32[64,512]{1,0:T(8,128)S(1)}, f32[64,512]{1,0:T(8,128)S(1)}, u32[]{:S(2)}, u32[]{:S(2)}) collective-permute-start(f32[64,512]{1,0:T(8,128)S(1)} %convolution_add_fusion.4), channel_id=1, source_target_pairs={{1,0},{2,1},{3,2},{4,3},{5,4},{6,5},{7,6},{8,7},{9,8},{10,9},{11,1... | collective-permute-start | bytes 393224 | tf_op jit(solution)/shard_map/while/body/eval_jaxpr/ppermute | solution.py:15
  275.1 6.5 %collective-permute-start = (f32[64,512]{1,0:T(8,128)S(1)}, f32[64,512]{1,0:T(8,128)S(1)}, u32[]{:S(2)}, u32[]{:S(2)}) collective-permute-start(f32[64,512]{1,0:T(8,128)S(1)} %convolution_add_fusion.4), channel_id=1, source_target_pairs={{1,0},{2,1},{3,2},{4,3},{5,4},{6,5},{7,6},{8,7},{9,8},{10,9},{11,1... | collective-permute-start | bytes 393224 | tf_op jit(solution)/shard_map/while/body/eval_jaxpr/ppermute | solution.py:15
  284.8 6.5 %collective-permute-start = (f32[64,512]{1,0:T(8,128)S(1)}, f32[64,512]{1,0:T(8,128)S(1)}, u32[]{:S(2)}, u32[]{:S(2)}) collective-permute-start(f32[64,512]{1,0:T(8,128)S(1)} %convolution_add_fusion.4), channel_id=1, source_target_pairs={{1,0},{2,1},{3,2},{4,3},{5,4},{6,5},{7,6},{8,7},{9,8},{10,9},{11,1... | collective-permute-start | bytes 393224 | tf_op jit(solution)/shard_map/while/body/eval_jaxpr/ppermute | solution.py:15
  291.3 2.8 collective-permute-done
  294.8 6.5 %collective-permute-start = (f32[64,512]{1,0:T(8,128)S(1)}, f32[64,512]{1,0:T(8,128)S(1)}, u32[]{:S(2)}, u32[]{:S(2)}) collective-permute-start(f32[64,512]{1,0:T(8,128)S(1)} %convolution_add_fusion.4), channel_id=1, source_target_pairs={{1,0},{2,1},{3,2},{4,3},{5,4},{6,5},{7,6},{8,7},{9,8},{10,9},{11,1... | collective-permute-start | bytes 393224 | tf_op jit(solution)/shard_map/while/body/eval_jaxpr/ppermute | solution.py:15
  301.3 3.8 collective-permute-done
  306.0 6.5 %collective-permute-start = (f32[64,512]{1,0:T(8,128)S(1)}, f32[64,512]{1,0:T(8,128)S(1)}, u32[]{:S(2)}, u32[]{:S(2)}) collective-permute-start(f32[64,512]{1,0:T(8,128)S(1)} %convolution_add_fusion.4), channel_id=1, source_target_pairs={{1,0},{2,1},{3,2},{4,3},{5,4},{6,5},{7,6},{8,7},{9,8},{10,9},{11,1... | collective-permute-start | bytes 393224 | tf_op jit(solution)/shard_map/while/body/eval_jaxpr/ppermute | solution.py:15
  312.5 3.0 collective-permute-done
  316.2 6.5 %collective-permute-start = (f32[64,512]{1,0:T(8,128)S(1)}, f32[64,512]{1,0:T(8,128)S(1)}, u32[]{:S(2)}, u32[]{:S(2)}) collective-permute-start(f32[64,512]{1,0:T(8,128)S(1)} %convolution_add_fusion.4), channel_id=1, source_target_pairs={{1,0},{2,1},{3,2},{4,3},{5,4},{6,5},{7,6},{8,7},{9,8},{10,9},{11,1... | collective-permute-start | bytes 393224 | tf_op jit(solution)/shard_map/while/body/eval_jaxpr/ppermute | solution.py:15
  326.0 6.5 %collective-permute-start = (f32[64,512]{1,0:T(8,128)S(1)}, f32[64,512]{1,0:T(8,128)S(1)}, u32[]{:S(2)}, u32[]{:S(2)}) collective-permute-start(f32[64,512]{1,0:T(8,128)S(1)} %convolution_add_fusion.4), channel_id=1, source_target_pairs={{1,0},{2,1},{3,2},{4,3},{5,4},{6,5},{7,6},{8,7},{9,8},{10,9},{11,1... | collective-permute-start | bytes 393224 | tf_op jit(solution)/shard_map/while/body/eval_jaxpr/ppermute | solution.py:15
  335.8 6.5 %collective-permute-start = (f32[64,512]{1,0:T(8,128)S(1)}, f32[64,512]{1,0:T(8,128)S(1)}, u32[]{:S(2)}, u32[]{:S(2)}) collective-permute-start(f32[64,512]{1,0:T(8,128)S(1)} %convolution_add_fusion.4), channel_id=1, source_target_pairs={{1,0},{2,1},{3,2},{4,3},{5,4},{6,5},{7,6},{8,7},{9,8},{10,9},{11,1... | collective-permute-start | bytes 393224 | tf_op jit(solution)/shard_map/while/body/eval_jaxpr/ppermute | solution.py:15
  345.5 6.5 %collective-permute-start = (f32[64,512]{1,0:T(8,128)S(1)}, f32[64,512]{1,0:T(8,128)S(1)}, u32[]{:S(2)}, u32[]{:S(2)}) collective-permute-start(f32[64,512]{1,0:T(8,128)S(1)} %convolution_add_fusion.4), channel_id=1, source_target_pairs={{1,0},{2,1},{3,2},{4,3},{5,4},{6,5},{7,6},{8,7},{9,8},{10,9},{11,1... | collective-permute-start | bytes 393224 | tf_op jit(solution)/shard_map/while/body/eval_jaxpr/ppermute | solution.py:15
  355.3 6.5 %collective-permute-start = (f32[64,512]{1,0:T(8,128)S(1)}, f32[64,512]{1,0:T(8,128)S(1)}, u32[]{:S(2)}, u32[]{:S(2)}) collective-permute-start(f32[64,512]{1,0:T(8,128)S(1)} %convolution_add_fusion.4), channel_id=1, source_target_pairs={{1,0},{2,1},{3,2},{4,3},{5,4},{6,5},{7,6},{8,7},{9,8},{10,9},{11,1... | collective-permute-start | bytes 393224 | tf_op jit(solution)/shard_map/while/body/eval_jaxpr/ppermute | solution.py:15
  365.0 6.5 %collective-permute-start = (f32[64,512]{1,0:T(8,128)S(1)}, f32[64,512]{1,0:T(8,128)S(1)}, u32[]{:S(2)}, u32[]{:S(2)}) collective-permute-start(f32[64,512]{1,0:T(8,128)S(1)} %convolution_add_fusion.4), channel_id=1, source_target_pairs={{1,0},{2,1},{3,2},{4,3},{5,4},{6,5},{7,6},{8,7},{9,8},{10,9},{11,1... | collective-permute-start | bytes 393224 | tf_op jit(solution)/shard_map/while/body/eval_jaxpr/ppermute | solution.py:15
  371.5 2.8 collective-permute-done
  375.1 6.5 %collective-permute-start = (f32[64,512]{1,0:T(8,128)S(1)}, f32[64,512]{1,0:T(8,128)S(1)}, u32[]{:S(2)}, u32[]{:S(2)}) collective-permute-start(f32[64,512]{1,0:T(8,128)S(1)} %convolution_add_fusion.4), channel_id=1, source_target_pairs={{1,0},{2,1},{3,2},{4,3},{5,4},{6,5},{7,6},{8,7},{9,8},{10,9},{11,1... | collective-permute-start | bytes 393224 | tf_op jit(solution)/shard_map/while/body/eval_jaxpr/ppermute | solution.py:15
  381.6 3.9 collective-permute-done
  386.2 6.5 %collective-permute-start = (f32[64,512]{1,0:T(8,128)S(1)}, f32[64,512]{1,0:T(8,128)S(1)}, u32[]{:S(2)}, u32[]{:S(2)}) collective-permute-start(f32[64,512]{1,0:T(8,128)S(1)} %convolution_add_fusion.4), channel_id=1, source_target_pairs={{1,0},{2,1},{3,2},{4,3},{5,4},{6,5},{7,6},{8,7},{9,8},{10,9},{11,1... | collective-permute-start | bytes 393224 | tf_op jit(solution)/shard_map/while/body/eval_jaxpr/ppermute | solution.py:15
  392.7 3.0 collective-permute-done
  396.4 6.5 %collective-permute-start = (f32[64,512]{1,0:T(8,128)S(1)}, f32[64,512]{1,0:T(8,128)S(1)}, u32[]{:S(2)}, u32[]{:S(2)}) collective-permute-start(f32[64,512]{1,0:T(8,128)S(1)} %convolution_add_fusion.4), channel_id=1, source_target_pairs={{1,0},{2,1},{3,2},{4,3},{5,4},{6,5},{7,6},{8,7},{9,8},{10,9},{11,1... | collective-permute-start | bytes 393224 | tf_op jit(solution)/shard_map/while/body/eval_jaxpr/ppermute | solution.py:15
  406.2 6.5 %collective-permute-start = (f32[64,512]{1,0:T(8,128)S(1)}, f32[64,512]{1,0:T(8,128)S(1)}, u32[]{:S(2)}, u32[]{:S(2)}) collective-permute-start(f32[64,512]{1,0:T(8,128)S(1)} %convolution_add_fusion.4), channel_id=1, source_target_pairs={{1,0},{2,1},{3,2},{4,3},{5,4},{6,5},{7,6},{8,7},{9,8},{10,9},{11,1... | collective-permute-start | bytes 393224 | tf_op jit(solution)/shard_map/while/body/eval_jaxpr/ppermute | solution.py:15
  416.0 6.5 %collective-permute-start = (f32[64,512]{1,0:T(8,128)S(1)}, f32[64,512]{1,0:T(8,128)S(1)}, u32[]{:S(2)}, u32[]{:S(2)}) collective-permute-start(f32[64,512]{1,0:T(8,128)S(1)} %convolution_add_fusion.4), channel_id=1, source_target_pairs={{1,0},{2,1},{3,2},{4,3},{5,4},{6,5},{7,6},{8,7},{9,8},{10,9},{11,1... | collective-permute-start | bytes 393224 | tf_op jit(solution)/shard_map/while/body/eval_jaxpr/ppermute | solution.py:15
  425.8 6.5 %collective-permute-start = (f32[64,512]{1,0:T(8,128)S(1)}, f32[64,512]{1,0:T(8,128)S(1)}, u32[]{:S(2)}, u32[]{:S(2)}) collective-permute-start(f32[64,512]{1,0:T(8,128)S(1)} %convolution_add_fusion.4), channel_id=1, source_target_pairs={{1,0},{2,1},{3,2},{4,3},{5,4},{6,5},{7,6},{8,7},{9,8},{10,9},{11,1... | collective-permute-start | bytes 393224 | tf_op jit(solution)/shard_map/while/body/eval_jaxpr/ppermute | solution.py:15
  435.5 6.5 %collective-permute-start = (f32[64,512]{1,0:T(8,128)S(1)}, f32[64,512]{1,0:T(8,128)S(1)}, u32[]{:S(2)}, u32[]{:S(2)}) collective-permute-start(f32[64,512]{1,0:T(8,128)S(1)} %convolution_add_fusion.4), channel_id=1, source_target_pairs={{1,0},{2,1},{3,2},{4,3},{5,4},{6,5},{7,6},{8,7},{9,8},{10,9},{11,1... | collective-permute-start | bytes 393224 | tf_op jit(solution)/shard_map/while/body/eval_jaxpr/ppermute | solution.py:15
  (101 shorter events, 73.8 us)
Async XLA Ops:
  7.2 438.8 %copy-start = (f32[1,1,64,512]{3,2,1,0:T(8,128)S(1)}, f32[1,1,64,512]{3,2,1,0:T(8,128)}, u32[]{:S(2)}) copy-start(f32[1,1,64,512]{3,2,1,0:T(8,128)} %param.10) | copy-start | bytes 393220
  7.2 123.5 %all-reduce.2.cloned.1.call-start = ((), (), s32[]{:S(2)}) async-start(), calls=%async_computation | async-start | bytes 1048576 | tf_op jit(solution)/shard_map/psum | solution.py:27
  9.6 0.9 copy-start.4
  9.6 121.1 %copy-start.2 = (s32[1,1,32,2048]{3,2,1,0:T(8,128)S(1)}, s32[1,1,32,2048]{3,2,1,0:T(8,128)}, u32[]{:S(2)}) copy-start(s32[1,1,32,2048]{3,2,1,0:T(8,128)} %param.13) | copy-start | bytes 786436
  9.7 122.8 %copy-start.1 = (f32[1,1,512,512]{3,2,1,0:T(8,128)S(1)}, f32[1,1,512,512]{3,2,1,0:T(8,128)}, u32[]{:S(2)}) copy-start(f32[1,1,512,512]{3,2,1,0:T(8,128)} %param.9) | copy-start | bytes 3145732
  132.3 0.9 copy-start.3
  132.4 0.9 copy-start.5
  134.8 10.0 %collective-permute-start = (f32[64,512]{1,0:T(8,128)S(1)}, f32[64,512]{1,0:T(8,128)S(1)}, u32[]{:S(2)}, u32[]{:S(2)}) collective-permute-start(f32[64,512]{1,0:T(8,128)S(1)} %convolution_add_fusion.4), channel_id=1, source_target_pairs={{1,0},{2,1},{3,2},{4,3},{5,4},{6,5},{7,6},{8,7},{9,8},{10,9},{11,1... | collective-permute-start | bytes 393224 | tf_op jit(solution)/shard_map/while/body/eval_jaxpr/ppermute | solution.py:15
  145.5 9.4 %collective-permute-start = (f32[64,512]{1,0:T(8,128)S(1)}, f32[64,512]{1,0:T(8,128)S(1)}, u32[]{:S(2)}, u32[]{:S(2)}) collective-permute-start(f32[64,512]{1,0:T(8,128)S(1)} %convolution_add_fusion.4), channel_id=1, source_target_pairs={{1,0},{2,1},{3,2},{4,3},{5,4},{6,5},{7,6},{8,7},{9,8},{10,9},{11,1... | collective-permute-start | bytes 393224 | tf_op jit(solution)/shard_map/while/body/eval_jaxpr/ppermute | solution.py:15
  155.8 9.0 %collective-permute-start = (f32[64,512]{1,0:T(8,128)S(1)}, f32[64,512]{1,0:T(8,128)S(1)}, u32[]{:S(2)}, u32[]{:S(2)}) collective-permute-start(f32[64,512]{1,0:T(8,128)S(1)} %convolution_add_fusion.4), channel_id=1, source_target_pairs={{1,0},{2,1},{3,2},{4,3},{5,4},{6,5},{7,6},{8,7},{9,8},{10,9},{11,1... | collective-permute-start | bytes 393224 | tf_op jit(solution)/shard_map/while/body/eval_jaxpr/ppermute | solution.py:15
  165.6 9.0 %collective-permute-start = (f32[64,512]{1,0:T(8,128)S(1)}, f32[64,512]{1,0:T(8,128)S(1)}, u32[]{:S(2)}, u32[]{:S(2)}) collective-permute-start(f32[64,512]{1,0:T(8,128)S(1)} %convolution_add_fusion.4), channel_id=1, source_target_pairs={{1,0},{2,1},{3,2},{4,3},{5,4},{6,5},{7,6},{8,7},{9,8},{10,9},{11,1... | collective-permute-start | bytes 393224 | tf_op jit(solution)/shard_map/while/body/eval_jaxpr/ppermute | solution.py:15
  175.3 9.0 %collective-permute-start = (f32[64,512]{1,0:T(8,128)S(1)}, f32[64,512]{1,0:T(8,128)S(1)}, u32[]{:S(2)}, u32[]{:S(2)}) collective-permute-start(f32[64,512]{1,0:T(8,128)S(1)} %convolution_add_fusion.4), channel_id=1, source_target_pairs={{1,0},{2,1},{3,2},{4,3},{5,4},{6,5},{7,6},{8,7},{9,8},{10,9},{11,1... | collective-permute-start | bytes 393224 | tf_op jit(solution)/shard_map/while/body/eval_jaxpr/ppermute | solution.py:15
  185.1 9.0 %collective-permute-start = (f32[64,512]{1,0:T(8,128)S(1)}, f32[64,512]{1,0:T(8,128)S(1)}, u32[]{:S(2)}, u32[]{:S(2)}) collective-permute-start(f32[64,512]{1,0:T(8,128)S(1)} %convolution_add_fusion.4), channel_id=1, source_target_pairs={{1,0},{2,1},{3,2},{4,3},{5,4},{6,5},{7,6},{8,7},{9,8},{10,9},{11,1... | collective-permute-start | bytes 393224 | tf_op jit(solution)/shard_map/while/body/eval_jaxpr/ppermute | solution.py:15
  194.8 9.0 %collective-permute-start = (f32[64,512]{1,0:T(8,128)S(1)}, f32[64,512]{1,0:T(8,128)S(1)}, u32[]{:S(2)}, u32[]{:S(2)}) collective-permute-start(f32[64,512]{1,0:T(8,128)S(1)} %convolution_add_fusion.4), channel_id=1, source_target_pairs={{1,0},{2,1},{3,2},{4,3},{5,4},{6,5},{7,6},{8,7},{9,8},{10,9},{11,1... | collective-permute-start | bytes 393224 | tf_op jit(solution)/shard_map/while/body/eval_jaxpr/ppermute | solution.py:15
  204.6 9.2 %collective-permute-start = (f32[64,512]{1,0:T(8,128)S(1)}, f32[64,512]{1,0:T(8,128)S(1)}, u32[]{:S(2)}, u32[]{:S(2)}) collective-permute-start(f32[64,512]{1,0:T(8,128)S(1)} %convolution_add_fusion.4), channel_id=1, source_target_pairs={{1,0},{2,1},{3,2},{4,3},{5,4},{6,5},{7,6},{8,7},{9,8},{10,9},{11,1... | collective-permute-start | bytes 393224 | tf_op jit(solution)/shard_map/while/body/eval_jaxpr/ppermute | solution.py:15
  214.6 10.4 %collective-permute-start = (f32[64,512]{1,0:T(8,128)S(1)}, f32[64,512]{1,0:T(8,128)S(1)}, u32[]{:S(2)}, u32[]{:S(2)}) collective-permute-start(f32[64,512]{1,0:T(8,128)S(1)} %convolution_add_fusion.4), channel_id=1, source_target_pairs={{1,0},{2,1},{3,2},{4,3},{5,4},{6,5},{7,6},{8,7},{9,8},{10,9},{11,1... | collective-permute-start | bytes 393224 | tf_op jit(solution)/shard_map/while/body/eval_jaxpr/ppermute | solution.py:15
  225.8 9.4 %collective-permute-start = (f32[64,512]{1,0:T(8,128)S(1)}, f32[64,512]{1,0:T(8,128)S(1)}, u32[]{:S(2)}, u32[]{:S(2)}) collective-permute-start(f32[64,512]{1,0:T(8,128)S(1)} %convolution_add_fusion.4), channel_id=1, source_target_pairs={{1,0},{2,1},{3,2},{4,3},{5,4},{6,5},{7,6},{8,7},{9,8},{10,9},{11,1... | collective-permute-start | bytes 393224 | tf_op jit(solution)/shard_map/while/body/eval_jaxpr/ppermute | solution.py:15
  236.0 9.0 %collective-permute-start = (f32[64,512]{1,0:T(8,128)S(1)}, f32[64,512]{1,0:T(8,128)S(1)}, u32[]{:S(2)}, u32[]{:S(2)}) collective-permute-start(f32[64,512]{1,0:T(8,128)S(1)} %convolution_add_fusion.4), channel_id=1, source_target_pairs={{1,0},{2,1},{3,2},{4,3},{5,4},{6,5},{7,6},{8,7},{9,8},{10,9},{11,1... | collective-permute-start | bytes 393224 | tf_op jit(solution)/shard_map/while/body/eval_jaxpr/ppermute | solution.py:15
  245.8 9.0 %collective-permute-start = (f32[64,512]{1,0:T(8,128)S(1)}, f32[64,512]{1,0:T(8,128)S(1)}, u32[]{:S(2)}, u32[]{:S(2)}) collective-permute-start(f32[64,512]{1,0:T(8,128)S(1)} %convolution_add_fusion.4), channel_id=1, source_target_pairs={{1,0},{2,1},{3,2},{4,3},{5,4},{6,5},{7,6},{8,7},{9,8},{10,9},{11,1... | collective-permute-start | bytes 393224 | tf_op jit(solution)/shard_map/while/body/eval_jaxpr/ppermute | solution.py:15
  255.5 9.0 %collective-permute-start = (f32[64,512]{1,0:T(8,128)S(1)}, f32[64,512]{1,0:T(8,128)S(1)}, u32[]{:S(2)}, u32[]{:S(2)}) collective-permute-start(f32[64,512]{1,0:T(8,128)S(1)} %convolution_add_fusion.4), channel_id=1, source_target_pairs={{1,0},{2,1},{3,2},{4,3},{5,4},{6,5},{7,6},{8,7},{9,8},{10,9},{11,1... | collective-permute-start | bytes 393224 | tf_op jit(solution)/shard_map/while/body/eval_jaxpr/ppermute | solution.py:15
  265.3 9.0 %collective-permute-start = (f32[64,512]{1,0:T(8,128)S(1)}, f32[64,512]{1,0:T(8,128)S(1)}, u32[]{:S(2)}, u32[]{:S(2)}) collective-permute-start(f32[64,512]{1,0:T(8,128)S(1)} %convolution_add_fusion.4), channel_id=1, source_target_pairs={{1,0},{2,1},{3,2},{4,3},{5,4},{6,5},{7,6},{8,7},{9,8},{10,9},{11,1... | collective-permute-start | bytes 393224 | tf_op jit(solution)/shard_map/while/body/eval_jaxpr/ppermute | solution.py:15
  275.1 9.0 %collective-permute-start = (f32[64,512]{1,0:T(8,128)S(1)}, f32[64,512]{1,0:T(8,128)S(1)}, u32[]{:S(2)}, u32[]{:S(2)}) collective-permute-start(f32[64,512]{1,0:T(8,128)S(1)} %convolution_add_fusion.4), channel_id=1, source_target_pairs={{1,0},{2,1},{3,2},{4,3},{5,4},{6,5},{7,6},{8,7},{9,8},{10,9},{11,1... | collective-permute-start | bytes 393224 | tf_op jit(solution)/shard_map/while/body/eval_jaxpr/ppermute | solution.py:15
  284.8 9.2 %collective-permute-start = (f32[64,512]{1,0:T(8,128)S(1)}, f32[64,512]{1,0:T(8,128)S(1)}, u32[]{:S(2)}, u32[]{:S(2)}) collective-permute-start(f32[64,512]{1,0:T(8,128)S(1)} %convolution_add_fusion.4), channel_id=1, source_target_pairs={{1,0},{2,1},{3,2},{4,3},{5,4},{6,5},{7,6},{8,7},{9,8},{10,9},{11,1... | collective-permute-start | bytes 393224 | tf_op jit(solution)/shard_map/while/body/eval_jaxpr/ppermute | solution.py:15
  294.8 10.3 %collective-permute-start = (f32[64,512]{1,0:T(8,128)S(1)}, f32[64,512]{1,0:T(8,128)S(1)}, u32[]{:S(2)}, u32[]{:S(2)}) collective-permute-start(f32[64,512]{1,0:T(8,128)S(1)} %convolution_add_fusion.4), channel_id=1, source_target_pairs={{1,0},{2,1},{3,2},{4,3},{5,4},{6,5},{7,6},{8,7},{9,8},{10,9},{11,1... | collective-permute-start | bytes 393224 | tf_op jit(solution)/shard_map/while/body/eval_jaxpr/ppermute | solution.py:15
  306.0 9.5 %collective-permute-start = (f32[64,512]{1,0:T(8,128)S(1)}, f32[64,512]{1,0:T(8,128)S(1)}, u32[]{:S(2)}, u32[]{:S(2)}) collective-permute-start(f32[64,512]{1,0:T(8,128)S(1)} %convolution_add_fusion.4), channel_id=1, source_target_pairs={{1,0},{2,1},{3,2},{4,3},{5,4},{6,5},{7,6},{8,7},{9,8},{10,9},{11,1... | collective-permute-start | bytes 393224 | tf_op jit(solution)/shard_map/while/body/eval_jaxpr/ppermute | solution.py:15
  316.2 9.0 %collective-permute-start = (f32[64,512]{1,0:T(8,128)S(1)}, f32[64,512]{1,0:T(8,128)S(1)}, u32[]{:S(2)}, u32[]{:S(2)}) collective-permute-start(f32[64,512]{1,0:T(8,128)S(1)} %convolution_add_fusion.4), channel_id=1, source_target_pairs={{1,0},{2,1},{3,2},{4,3},{5,4},{6,5},{7,6},{8,7},{9,8},{10,9},{11,1... | collective-permute-start | bytes 393224 | tf_op jit(solution)/shard_map/while/body/eval_jaxpr/ppermute | solution.py:15
  326.0 9.0 %collective-permute-start = (f32[64,512]{1,0:T(8,128)S(1)}, f32[64,512]{1,0:T(8,128)S(1)}, u32[]{:S(2)}, u32[]{:S(2)}) collective-permute-start(f32[64,512]{1,0:T(8,128)S(1)} %convolution_add_fusion.4), channel_id=1, source_target_pairs={{1,0},{2,1},{3,2},{4,3},{5,4},{6,5},{7,6},{8,7},{9,8},{10,9},{11,1... | collective-permute-start | bytes 393224 | tf_op jit(solution)/shard_map/while/body/eval_jaxpr/ppermute | solution.py:15
  335.8 9.0 %collective-permute-start = (f32[64,512]{1,0:T(8,128)S(1)}, f32[64,512]{1,0:T(8,128)S(1)}, u32[]{:S(2)}, u32[]{:S(2)}) collective-permute-start(f32[64,512]{1,0:T(8,128)S(1)} %convolution_add_fusion.4), channel_id=1, source_target_pairs={{1,0},{2,1},{3,2},{4,3},{5,4},{6,5},{7,6},{8,7},{9,8},{10,9},{11,1... | collective-permute-start | bytes 393224 | tf_op jit(solution)/shard_map/while/body/eval_jaxpr/ppermute | solution.py:15
  345.5 9.0 %collective-permute-start = (f32[64,512]{1,0:T(8,128)S(1)}, f32[64,512]{1,0:T(8,128)S(1)}, u32[]{:S(2)}, u32[]{:S(2)}) collective-permute-start(f32[64,512]{1,0:T(8,128)S(1)} %convolution_add_fusion.4), channel_id=1, source_target_pairs={{1,0},{2,1},{3,2},{4,3},{5,4},{6,5},{7,6},{8,7},{9,8},{10,9},{11,1... | collective-permute-start | bytes 393224 | tf_op jit(solution)/shard_map/while/body/eval_jaxpr/ppermute | solution.py:15
  355.3 9.0 %collective-permute-start = (f32[64,512]{1,0:T(8,128)S(1)}, f32[64,512]{1,0:T(8,128)S(1)}, u32[]{:S(2)}, u32[]{:S(2)}) collective-permute-start(f32[64,512]{1,0:T(8,128)S(1)} %convolution_add_fusion.4), channel_id=1, source_target_pairs={{1,0},{2,1},{3,2},{4,3},{5,4},{6,5},{7,6},{8,7},{9,8},{10,9},{11,1... | collective-permute-start | bytes 393224 | tf_op jit(solution)/shard_map/while/body/eval_jaxpr/ppermute | solution.py:15
  365.0 9.2 %collective-permute-start = (f32[64,512]{1,0:T(8,128)S(1)}, f32[64,512]{1,0:T(8,128)S(1)}, u32[]{:S(2)}, u32[]{:S(2)}) collective-permute-start(f32[64,512]{1,0:T(8,128)S(1)} %convolution_add_fusion.4), channel_id=1, source_target_pairs={{1,0},{2,1},{3,2},{4,3},{5,4},{6,5},{7,6},{8,7},{9,8},{10,9},{11,1... | collective-permute-start | bytes 393224 | tf_op jit(solution)/shard_map/while/body/eval_jaxpr/ppermute | solution.py:15
  375.1 10.4 %collective-permute-start = (f32[64,512]{1,0:T(8,128)S(1)}, f32[64,512]{1,0:T(8,128)S(1)}, u32[]{:S(2)}, u32[]{:S(2)}) collective-permute-start(f32[64,512]{1,0:T(8,128)S(1)} %convolution_add_fusion.4), channel_id=1, source_target_pairs={{1,0},{2,1},{3,2},{4,3},{5,4},{6,5},{7,6},{8,7},{9,8},{10,9},{11,1... | collective-permute-start | bytes 393224 | tf_op jit(solution)/shard_map/while/body/eval_jaxpr/ppermute | solution.py:15
  386.2 9.4 %collective-permute-start = (f32[64,512]{1,0:T(8,128)S(1)}, f32[64,512]{1,0:T(8,128)S(1)}, u32[]{:S(2)}, u32[]{:S(2)}) collective-permute-start(f32[64,512]{1,0:T(8,128)S(1)} %convolution_add_fusion.4), channel_id=1, source_target_pairs={{1,0},{2,1},{3,2},{4,3},{5,4},{6,5},{7,6},{8,7},{9,8},{10,9},{11,1... | collective-permute-start | bytes 393224 | tf_op jit(solution)/shard_map/while/body/eval_jaxpr/ppermute | solution.py:15
  396.4 9.0 %collective-permute-start = (f32[64,512]{1,0:T(8,128)S(1)}, f32[64,512]{1,0:T(8,128)S(1)}, u32[]{:S(2)}, u32[]{:S(2)}) collective-permute-start(f32[64,512]{1,0:T(8,128)S(1)} %convolution_add_fusion.4), channel_id=1, source_target_pairs={{1,0},{2,1},{3,2},{4,3},{5,4},{6,5},{7,6},{8,7},{9,8},{10,9},{11,1... | collective-permute-start | bytes 393224 | tf_op jit(solution)/shard_map/while/body/eval_jaxpr/ppermute | solution.py:15
  406.2 9.0 %collective-permute-start = (f32[64,512]{1,0:T(8,128)S(1)}, f32[64,512]{1,0:T(8,128)S(1)}, u32[]{:S(2)}, u32[]{:S(2)}) collective-permute-start(f32[64,512]{1,0:T(8,128)S(1)} %convolution_add_fusion.4), channel_id=1, source_target_pairs={{1,0},{2,1},{3,2},{4,3},{5,4},{6,5},{7,6},{8,7},{9,8},{10,9},{11,1... | collective-permute-start | bytes 393224 | tf_op jit(solution)/shard_map/while/body/eval_jaxpr/ppermute | solution.py:15
  416.0 9.0 %collective-permute-start = (f32[64,512]{1,0:T(8,128)S(1)}, f32[64,512]{1,0:T(8,128)S(1)}, u32[]{:S(2)}, u32[]{:S(2)}) collective-permute-start(f32[64,512]{1,0:T(8,128)S(1)} %convolution_add_fusion.4), channel_id=1, source_target_pairs={{1,0},{2,1},{3,2},{4,3},{5,4},{6,5},{7,6},{8,7},{9,8},{10,9},{11,1... | collective-permute-start | bytes 393224 | tf_op jit(solution)/shard_map/while/body/eval_jaxpr/ppermute | solution.py:15
  425.8 9.0 %collective-permute-start = (f32[64,512]{1,0:T(8,128)S(1)}, f32[64,512]{1,0:T(8,128)S(1)}, u32[]{:S(2)}, u32[]{:S(2)}) collective-permute-start(f32[64,512]{1,0:T(8,128)S(1)} %convolution_add_fusion.4), channel_id=1, source_target_pairs={{1,0},{2,1},{3,2},{4,3},{5,4},{6,5},{7,6},{8,7},{9,8},{10,9},{11,1... | collective-permute-start | bytes 393224 | tf_op jit(solution)/shard_map/while/body/eval_jaxpr/ppermute | solution.py:15
  435.5 9.0 %collective-permute-start = (f32[64,512]{1,0:T(8,128)S(1)}, f32[64,512]{1,0:T(8,128)S(1)}, u32[]{:S(2)}, u32[]{:S(2)}) collective-permute-start(f32[64,512]{1,0:T(8,128)S(1)} %convolution_add_fusion.4), channel_id=1, source_target_pairs={{1,0},{2,1},{3,2},{4,3},{5,4},{6,5},{7,6},{8,7},{9,8},{10,9},{11,1... | collective-permute-start | bytes 393224 | tf_op jit(solution)/shard_map/while/body/eval_jaxpr/ppermute | solution.py:15
Sparse Core Ops, SparseCore 0:
  10.9 119.8 all-reduce.1
where the time goes:
time: 456 us; the launch traced here: 455 us
  waiting for transfers between devices  206 us (45%)
  starting transfers between devices  200 us (44%)
  matrix products  31.3 us (7%)
  between operations  14.1 us (3%)
    ppermute x31, starting transfers between devices, from_behind(): return lax.ppermute(block, axis, route)  200 us
    psum x1, waiting for transfers between devices, shards(): landmark = lax.psum(partial_value, 'team')  120 us
    ppermute x31, waiting for transfers between devices, from_behind(): return lax.ppermute(block, axis, route)  85.5 us
    dot_general x33, matrix products, matmul(): return jnp.dot(left, right, precision=HIGHEST)  25.5 us
  transfers between devices with their start and end apart: 32, of which 32 were waited for; matrix products, arithmetic and copies ran while one was open for 0% of the time, Pallas kernels for 0%

commit v1 on v0

--- a/solution.py
+++ b/solution.py
@@ -24,7 +24,8 @@
     matrices = transitions[0]
     incident = incidence[0].astype(jnp.float32)
     partial_value = jnp.einsum("scr,srl->scl", measured[0], incident, precision=HIGHEST)
-    landmark = lax.psum(partial_value, "team")
+    _bind_node = lambda own_rows: jnp.sum(lax.all_gather(own_rows, axis_name="team"), 0)
+    landmark = _bind_node(partial_value)
     injection = jnp.einsum("scl,srl->scr", landmark, incident, precision=HIGHEST)
     driven = cotangent[0] + jnp.repeat(injection, STATES, axis=2) * obs_gain[0][None, None, :]
     offset = jnp.zeros((COLS, TEAM_STATES), jnp.float32)

time: 456 us -> 399 us (0.88)
  waiting for transfers between devices: 206 us -> 147 us
    psum x1 -> x0, waiting for transfers between devices: 120 us -> none  [shards(): landmark = lax.psum(partial_value, 'team')]
    all_gather x0 -> x1, waiting for transfers between devices: none -> 63.2 us  [shards(): lax.all_gather(own_rows, axis_name='team')]
where the time goes in v1:
time: 399 us; the launch traced here: 398 us
  starting transfers between devices  200 us (50%)
  waiting for transfers between devices  147 us (37%)
  matrix products  30.4 us (8%)
  between operations  14.2 us (4%)
  other arithmetic  4.55 us (1%)
    ppermute x31, starting transfers between devices, from_behind(): return lax.ppermute(block, axis, route)  200 us
    ppermute x31, waiting for transfers between devices, from_behind(): return lax.ppermute(block, axis, route)  84.1 us
    all_gather x1, waiting for transfers between devices, shards(): lax.all_gather(own_rows, axis_name='team')  63.2 us
    dot_general x33, matrix products, matmul(): return jnp.dot(left, right, precision=HIGHEST)  25.5 us
  transfers between devices with their start and end apart: 32, of which 32 were waited for; matrix products, arithmetic and copies ran while one was open for 0% of the time, Pallas kernels for 0%

profile of v1, /device:TPU:30, one launch (start us, length us, event | category | flops | bytes accessed | tf_op | source)
XLA Modules:
  0.0 397.7 jit_solution(16090007423280004034)
XLA Ops:
  9.8 63.2 %all-gather.3.cloned.1.call-done = f32[1024,2048]{1,0:T(8,128)} async-done(((f32[64,2048]{1,0:T(8,128)}), f32[1024,2048]{1,0:T(8,128)}) %all-gather.3.cloned.1.call-update) | async-done | bytes 8388624 | tf_op jit(solution)/shard_map/all_gather | solution.py:27
  73.0 3.9 reduce.1
  78.4 309.2 %while.10 = (s32[]{:T(128)}, f32[64,512]{1,0:T(8,128)S(1)}, f32[1,1,512,512]{3,2,1,0:T(8,128)S(1)}, f32[64,512]{1,0:T(8,128)S(1)}, f32[64,512]{1,0:T(8,128)S(1)}, /*index=5*/s32[]{:T(128)}) while((s32[]{:T(128)}, f32[64,512]{1,0:T(8,128)S(1)}, f32[1,1,512,512]{3,2,1,0:T(8,128)S(1)}, f32[64,512]{1,0:T(8,128)S(1)}, f32[64,512]{1,0:T(8,128)S(1)}, ...), condition=%wide.region_2.3_spmd, body=%wide.region_1.2_spmd.sunk | while | flops 201392128 | bytes 2359405 | solution.py:43
  79.2 6.1 %collective-permute-start = (f32[64,512]{1,0:T(8,128)S(1)}, f32[64,512]{1,0:T(8,128)S(1)}, u32[]{:S(2)}, u32[]{:S(2)}) collective-permute-start(f32[64,512]{1,0:T(8,128)S(1)} %convolution_add_fusion.4), channel_id=1, source_target_pairs={{1,0},{2,1},{3,2},{4,3},{5,4},{6,5},{7,6},{8,7},{9,8},{10,9},{11,1... | collective-permute-start | bytes 393224 | tf_op jit(solution)/shard_map/while/body/eval_jaxpr/ppermute | solution.py:15
  85.4 3.1 collective-permute-done
  89.3 6.5 %collective-permute-start = (f32[64,512]{1,0:T(8,128)S(1)}, f32[64,512]{1,0:T(8,128)S(1)}, u32[]{:S(2)}, u32[]{:S(2)}) collective-permute-start(f32[64,512]{1,0:T(8,128)S(1)} %convolution_add_fusion.4), channel_id=1, source_target_pairs={{1,0},{2,1},{3,2},{4,3},{5,4},{6,5},{7,6},{8,7},{9,8},{10,9},{11,1... | collective-permute-start | bytes 393224 | tf_op jit(solution)/shard_map/while/body/eval_jaxpr/ppermute | solution.py:15
  99.1 6.5 %collective-permute-start = (f32[64,512]{1,0:T(8,128)S(1)}, f32[64,512]{1,0:T(8,128)S(1)}, u32[]{:S(2)}, u32[]{:S(2)}) collective-permute-start(f32[64,512]{1,0:T(8,128)S(1)} %convolution_add_fusion.4), channel_id=1, source_target_pairs={{1,0},{2,1},{3,2},{4,3},{5,4},{6,5},{7,6},{8,7},{9,8},{10,9},{11,1... | collective-permute-start | bytes 393224 | tf_op jit(solution)/shard_map/while/body/eval_jaxpr/ppermute | solution.py:15
  105.5 2.5 collective-permute-done
  108.8 6.5 %collective-permute-start = (f32[64,512]{1,0:T(8,128)S(1)}, f32[64,512]{1,0:T(8,128)S(1)}, u32[]{:S(2)}, u32[]{:S(2)}) collective-permute-start(f32[64,512]{1,0:T(8,128)S(1)} %convolution_add_fusion.4), channel_id=1, source_target_pairs={{1,0},{2,1},{3,2},{4,3},{5,4},{6,5},{7,6},{8,7},{9,8},{10,9},{11,1... | collective-permute-start | bytes 393224 | tf_op jit(solution)/shard_map/while/body/eval_jaxpr/ppermute | solution.py:15
  115.3 2.5 collective-permute-done
  118.6 6.5 %collective-permute-start = (f32[64,512]{1,0:T(8,128)S(1)}, f32[64,512]{1,0:T(8,128)S(1)}, u32[]{:S(2)}, u32[]{:S(2)}) collective-permute-start(f32[64,512]{1,0:T(8,128)S(1)} %convolution_add_fusion.4), channel_id=1, source_target_pairs={{1,0},{2,1},{3,2},{4,3},{5,4},{6,5},{7,6},{8,7},{9,8},{10,9},{11,1... | collective-permute-start | bytes 393224 | tf_op jit(solution)/shard_map/while/body/eval_jaxpr/ppermute | solution.py:15
  125.1 2.5 collective-permute-done
  128.3 6.5 %collective-permute-start = (f32[64,512]{1,0:T(8,128)S(1)}, f32[64,512]{1,0:T(8,128)S(1)}, u32[]{:S(2)}, u32[]{:S(2)}) collective-permute-start(f32[64,512]{1,0:T(8,128)S(1)} %convolution_add_fusion.4), channel_id=1, source_target_pairs={{1,0},{2,1},{3,2},{4,3},{5,4},{6,5},{7,6},{8,7},{9,8},{10,9},{11,1... | collective-permute-start | bytes 393224 | tf_op jit(solution)/shard_map/while/body/eval_jaxpr/ppermute | solution.py:15
  134.8 2.5 collective-permute-done
  138.1 6.5 %collective-permute-start = (f32[64,512]{1,0:T(8,128)S(1)}, f32[64,512]{1,0:T(8,128)S(1)}, u32[]{:S(2)}, u32[]{:S(2)}) collective-permute-start(f32[64,512]{1,0:T(8,128)S(1)} %convolution_add_fusion.4), channel_id=1, source_target_pairs={{1,0},{2,1},{3,2},{4,3},{5,4},{6,5},{7,6},{8,7},{9,8},{10,9},{11,1... | collective-permute-start | bytes 393224 | tf_op jit(solution)/shard_map/while/body/eval_jaxpr/ppermute | solution.py:15
  144.6 2.6 collective-permute-done
  148.0 6.5 %collective-permute-start = (f32[64,512]{1,0:T(8,128)S(1)}, f32[64,512]{1,0:T(8,128)S(1)}, u32[]{:S(2)}, u32[]{:S(2)}) collective-permute-start(f32[64,512]{1,0:T(8,128)S(1)} %convolution_add_fusion.4), channel_id=1, source_target_pairs={{1,0},{2,1},{3,2},{4,3},{5,4},{6,5},{7,6},{8,7},{9,8},{10,9},{11,1... | collective-permute-start | bytes 393224 | tf_op jit(solution)/shard_map/while/body/eval_jaxpr/ppermute | solution.py:15
  154.5 3.7 collective-permute-done
  159.0 6.5 %collective-permute-start = (f32[64,512]{1,0:T(8,128)S(1)}, f32[64,512]{1,0:T(8,128)S(1)}, u32[]{:S(2)}, u32[]{:S(2)}) collective-permute-start(f32[64,512]{1,0:T(8,128)S(1)} %convolution_add_fusion.4), channel_id=1, source_target_pairs={{1,0},{2,1},{3,2},{4,3},{5,4},{6,5},{7,6},{8,7},{9,8},{10,9},{11,1... | collective-permute-start | bytes 393224 | tf_op jit(solution)/shard_map/while/body/eval_jaxpr/ppermute | solution.py:15
  165.5 3.0 collective-permute-done
  169.3 6.5 %collective-permute-start = (f32[64,512]{1,0:T(8,128)S(1)}, f32[64,512]{1,0:T(8,128)S(1)}, u32[]{:S(2)}, u32[]{:S(2)}) collective-permute-start(f32[64,512]{1,0:T(8,128)S(1)} %convolution_add_fusion.4), channel_id=1, source_target_pairs={{1,0},{2,1},{3,2},{4,3},{5,4},{6,5},{7,6},{8,7},{9,8},{10,9},{11,1... | collective-permute-start | bytes 393224 | tf_op jit(solution)/shard_map/while/body/eval_jaxpr/ppermute | solution.py:15
  179.1 6.5 %collective-permute-start = (f32[64,512]{1,0:T(8,128)S(1)}, f32[64,512]{1,0:T(8,128)S(1)}, u32[]{:S(2)}, u32[]{:S(2)}) collective-permute-start(f32[64,512]{1,0:T(8,128)S(1)} %convolution_add_fusion.4), channel_id=1, source_target_pairs={{1,0},{2,1},{3,2},{4,3},{5,4},{6,5},{7,6},{8,7},{9,8},{10,9},{11,1... | collective-permute-start | bytes 393224 | tf_op jit(solution)/shard_map/while/body/eval_jaxpr/ppermute | solution.py:15
  188.9 6.5 %collective-permute-start = (f32[64,512]{1,0:T(8,128)S(1)}, f32[64,512]{1,0:T(8,128)S(1)}, u32[]{:S(2)}, u32[]{:S(2)}) collective-permute-start(f32[64,512]{1,0:T(8,128)S(1)} %convolution_add_fusion.4), channel_id=1, source_target_pairs={{1,0},{2,1},{3,2},{4,3},{5,4},{6,5},{7,6},{8,7},{9,8},{10,9},{11,1... | collective-permute-start | bytes 393224 | tf_op jit(solution)/shard_map/while/body/eval_jaxpr/ppermute | solution.py:15
  198.6 6.5 %collective-permute-start = (f32[64,512]{1,0:T(8,128)S(1)}, f32[64,512]{1,0:T(8,128)S(1)}, u32[]{:S(2)}, u32[]{:S(2)}) collective-permute-start(f32[64,512]{1,0:T(8,128)S(1)} %convolution_add_fusion.4), channel_id=1, source_target_pairs={{1,0},{2,1},{3,2},{4,3},{5,4},{6,5},{7,6},{8,7},{9,8},{10,9},{11,1... | collective-permute-start | bytes 393224 | tf_op jit(solution)/shard_map/while/body/eval_jaxpr/ppermute | solution.py:15
  208.4 6.5 %collective-permute-start = (f32[64,512]{1,0:T(8,128)S(1)}, f32[64,512]{1,0:T(8,128)S(1)}, u32[]{:S(2)}, u32[]{:S(2)}) collective-permute-start(f32[64,512]{1,0:T(8,128)S(1)} %convolution_add_fusion.4), channel_id=1, source_target_pairs={{1,0},{2,1},{3,2},{4,3},{5,4},{6,5},{7,6},{8,7},{9,8},{10,9},{11,1... | collective-permute-start | bytes 393224 | tf_op jit(solution)/shard_map/while/body/eval_jaxpr/ppermute | solution.py:15
  218.1 6.5 %collective-permute-start = (f32[64,512]{1,0:T(8,128)S(1)}, f32[64,512]{1,0:T(8,128)S(1)}, u32[]{:S(2)}, u32[]{:S(2)}) collective-permute-start(f32[64,512]{1,0:T(8,128)S(1)} %convolution_add_fusion.4), channel_id=1, source_target_pairs={{1,0},{2,1},{3,2},{4,3},{5,4},{6,5},{7,6},{8,7},{9,8},{10,9},{11,1... | collective-permute-start | bytes 393224 | tf_op jit(solution)/shard_map/while/body/eval_jaxpr/ppermute | solution.py:15
  224.6 2.7 collective-permute-done
  228.1 6.5 %collective-permute-start = (f32[64,512]{1,0:T(8,128)S(1)}, f32[64,512]{1,0:T(8,128)S(1)}, u32[]{:S(2)}, u32[]{:S(2)}) collective-permute-start(f32[64,512]{1,0:T(8,128)S(1)} %convolution_add_fusion.4), channel_id=1, source_target_pairs={{1,0},{2,1},{3,2},{4,3},{5,4},{6,5},{7,6},{8,7},{9,8},{10,9},{11,1... | collective-permute-start | bytes 393224 | tf_op jit(solution)/shard_map/while/body/eval_jaxpr/ppermute | solution.py:15
  234.6 3.9 collective-permute-done
  239.3 6.5 %collective-permute-start = (f32[64,512]{1,0:T(8,128)S(1)}, f32[64,512]{1,0:T(8,128)S(1)}, u32[]{:S(2)}, u32[]{:S(2)}) collective-permute-start(f32[64,512]{1,0:T(8,128)S(1)} %convolution_add_fusion.4), channel_id=1, source_target_pairs={{1,0},{2,1},{3,2},{4,3},{5,4},{6,5},{7,6},{8,7},{9,8},{10,9},{11,1... | collective-permute-start | bytes 393224 | tf_op jit(solution)/shard_map/while/body/eval_jaxpr/ppermute | solution.py:15
  245.8 3.0 collective-permute-done
  249.6 6.5 %collective-permute-start = (f32[64,512]{1,0:T(8,128)S(1)}, f32[64,512]{1,0:T(8,128)S(1)}, u32[]{:S(2)}, u32[]{:S(2)}) collective-permute-start(f32[64,512]{1,0:T(8,128)S(1)} %convolution_add_fusion.4), channel_id=1, source_target_pairs={{1,0},{2,1},{3,2},{4,3},{5,4},{6,5},{7,6},{8,7},{9,8},{10,9},{11,1... | collective-permute-start | bytes 393224 | tf_op jit(solution)/shard_map/while/body/eval_jaxpr/ppermute | solution.py:15
  259.4 6.5 %collective-permute-start = (f32[64,512]{1,0:T(8,128)S(1)}, f32[64,512]{1,0:T(8,128)S(1)}, u32[]{:S(2)}, u32[]{:S(2)}) collective-permute-start(f32[64,512]{1,0:T(8,128)S(1)} %convolution_add_fusion.4), channel_id=1, source_target_pairs={{1,0},{2,1},{3,2},{4,3},{5,4},{6,5},{7,6},{8,7},{9,8},{10,9},{11,1... | collective-permute-start | bytes 393224 | tf_op jit(solution)/shard_map/while/body/eval_jaxpr/ppermute | solution.py:15
  269.1 6.5 %collective-permute-start = (f32[64,512]{1,0:T(8,128)S(1)}, f32[64,512]{1,0:T(8,128)S(1)}, u32[]{:S(2)}, u32[]{:S(2)}) collective-permute-start(f32[64,512]{1,0:T(8,128)S(1)} %convolution_add_fusion.4), channel_id=1, source_target_pairs={{1,0},{2,1},{3,2},{4,3},{5,4},{6,5},{7,6},{8,7},{9,8},{10,9},{11,1... | collective-permute-start | bytes 393224 | tf_op jit(solution)/shard_map/while/body/eval_jaxpr/ppermute | solution.py:15
  278.9 6.5 %collective-permute-start = (f32[64,512]{1,0:T(8,128)S(1)}, f32[64,512]{1,0:T(8,128)S(1)}, u32[]{:S(2)}, u32[]{:S(2)}) collective-permute-start(f32[64,512]{1,0:T(8,128)S(1)} %convolution_add_fusion.4), channel_id=1, source_target_pairs={{1,0},{2,1},{3,2},{4,3},{5,4},{6,5},{7,6},{8,7},{9,8},{10,9},{11,1... | collective-permute-start | bytes 393224 | tf_op jit(solution)/shard_map/while/body/eval_jaxpr/ppermute | solution.py:15
  288.6 6.5 %collective-permute-start = (f32[64,512]{1,0:T(8,128)S(1)}, f32[64,512]{1,0:T(8,128)S(1)}, u32[]{:S(2)}, u32[]{:S(2)}) collective-permute-start(f32[64,512]{1,0:T(8,128)S(1)} %convolution_add_fusion.4), channel_id=1, source_target_pairs={{1,0},{2,1},{3,2},{4,3},{5,4},{6,5},{7,6},{8,7},{9,8},{10,9},{11,1... | collective-permute-start | bytes 393224 | tf_op jit(solution)/shard_map/while/body/eval_jaxpr/ppermute | solution.py:15
  298.4 6.5 %collective-permute-start = (f32[64,512]{1,0:T(8,128)S(1)}, f32[64,512]{1,0:T(8,128)S(1)}, u32[]{:S(2)}, u32[]{:S(2)}) collective-permute-start(f32[64,512]{1,0:T(8,128)S(1)} %convolution_add_fusion.4), channel_id=1, source_target_pairs={{1,0},{2,1},{3,2},{4,3},{5,4},{6,5},{7,6},{8,7},{9,8},{10,9},{11,1... | collective-permute-start | bytes 393224 | tf_op jit(solution)/shard_map/while/body/eval_jaxpr/ppermute | solution.py:15
  304.9 2.7 collective-permute-done
  308.4 6.5 %collective-permute-start = (f32[64,512]{1,0:T(8,128)S(1)}, f32[64,512]{1,0:T(8,128)S(1)}, u32[]{:S(2)}, u32[]{:S(2)}) collective-permute-start(f32[64,512]{1,0:T(8,128)S(1)} %convolution_add_fusion.4), channel_id=1, source_target_pairs={{1,0},{2,1},{3,2},{4,3},{5,4},{6,5},{7,6},{8,7},{9,8},{10,9},{11,1... | collective-permute-start | bytes 393224 | tf_op jit(solution)/shard_map/while/body/eval_jaxpr/ppermute | solution.py:15
  314.9 3.9 collective-permute-done
  319.5 6.5 %collective-permute-start = (f32[64,512]{1,0:T(8,128)S(1)}, f32[64,512]{1,0:T(8,128)S(1)}, u32[]{:S(2)}, u32[]{:S(2)}) collective-permute-start(f32[64,512]{1,0:T(8,128)S(1)} %convolution_add_fusion.4), channel_id=1, source_target_pairs={{1,0},{2,1},{3,2},{4,3},{5,4},{6,5},{7,6},{8,7},{9,8},{10,9},{11,1... | collective-permute-start | bytes 393224 | tf_op jit(solution)/shard_map/while/body/eval_jaxpr/ppermute | solution.py:15
  326.0 3.0 collective-permute-done
  329.8 6.5 %collective-permute-start = (f32[64,512]{1,0:T(8,128)S(1)}, f32[64,512]{1,0:T(8,128)S(1)}, u32[]{:S(2)}, u32[]{:S(2)}) collective-permute-start(f32[64,512]{1,0:T(8,128)S(1)} %convolution_add_fusion.4), channel_id=1, source_target_pairs={{1,0},{2,1},{3,2},{4,3},{5,4},{6,5},{7,6},{8,7},{9,8},{10,9},{11,1... | collective-permute-start | bytes 393224 | tf_op jit(solution)/shard_map/while/body/eval_jaxpr/ppermute | solution.py:15
  339.6 6.5 %collective-permute-start = (f32[64,512]{1,0:T(8,128)S(1)}, f32[64,512]{1,0:T(8,128)S(1)}, u32[]{:S(2)}, u32[]{:S(2)}) collective-permute-start(f32[64,512]{1,0:T(8,128)S(1)} %convolution_add_fusion.4), channel_id=1, source_target_pairs={{1,0},{2,1},{3,2},{4,3},{5,4},{6,5},{7,6},{8,7},{9,8},{10,9},{11,1... | collective-permute-start | bytes 393224 | tf_op jit(solution)/shard_map/while/body/eval_jaxpr/ppermute | solution.py:15
  349.4 6.5 %collective-permute-start = (f32[64,512]{1,0:T(8,128)S(1)}, f32[64,512]{1,0:T(8,128)S(1)}, u32[]{:S(2)}, u32[]{:S(2)}) collective-permute-start(f32[64,512]{1,0:T(8,128)S(1)} %convolution_add_fusion.4), channel_id=1, source_target_pairs={{1,0},{2,1},{3,2},{4,3},{5,4},{6,5},{7,6},{8,7},{9,8},{10,9},{11,1... | collective-permute-start | bytes 393224 | tf_op jit(solution)/shard_map/while/body/eval_jaxpr/ppermute | solution.py:15
  359.1 6.5 %collective-permute-start = (f32[64,512]{1,0:T(8,128)S(1)}, f32[64,512]{1,0:T(8,128)S(1)}, u32[]{:S(2)}, u32[]{:S(2)}) collective-permute-start(f32[64,512]{1,0:T(8,128)S(1)} %convolution_add_fusion.4), channel_id=1, source_target_pairs={{1,0},{2,1},{3,2},{4,3},{5,4},{6,5},{7,6},{8,7},{9,8},{10,9},{11,1... | collective-permute-start | bytes 393224 | tf_op jit(solution)/shard_map/while/body/eval_jaxpr/ppermute | solution.py:15
  368.9 6.5 %collective-permute-start = (f32[64,512]{1,0:T(8,128)S(1)}, f32[64,512]{1,0:T(8,128)S(1)}, u32[]{:S(2)}, u32[]{:S(2)}) collective-permute-start(f32[64,512]{1,0:T(8,128)S(1)} %convolution_add_fusion.4), channel_id=1, source_target_pairs={{1,0},{2,1},{3,2},{4,3},{5,4},{6,5},{7,6},{8,7},{9,8},{10,9},{11,1... | collective-permute-start | bytes 393224 | tf_op jit(solution)/shard_map/while/body/eval_jaxpr/ppermute | solution.py:15
  378.6 6.5 %collective-permute-start = (f32[64,512]{1,0:T(8,128)S(1)}, f32[64,512]{1,0:T(8,128)S(1)}, u32[]{:S(2)}, u32[]{:S(2)}) collective-permute-start(f32[64,512]{1,0:T(8,128)S(1)} %convolution_add_fusion.4), channel_id=1, source_target_pairs={{1,0},{2,1},{3,2},{4,3},{5,4},{6,5},{7,6},{8,7},{9,8},{10,9},{11,1... | collective-permute-start | bytes 393224 | tf_op jit(solution)/shard_map/while/body/eval_jaxpr/ppermute | solution.py:15
  (100 shorter events, 73.7 us)
Async XLA Ops:
  7.2 381.9 %copy-start = (f32[1,1,64,512]{3,2,1,0:T(8,128)S(1)}, f32[1,1,64,512]{3,2,1,0:T(8,128)}, u32[]{:S(2)}) copy-start(f32[1,1,64,512]{3,2,1,0:T(8,128)} %param.10) | copy-start | bytes 393220
  7.2 69.8 %copy-start.2 = (s32[1,1,32,2048]{3,2,1,0:T(8,128)S(1)}, s32[1,1,32,2048]{3,2,1,0:T(8,128)}, u32[]{:S(2)}) copy-start(s32[1,1,32,2048]{3,2,1,0:T(8,128)} %param.13) | copy-start | bytes 786436
  7.2 70.5 %copy-start.4 = (f32[1,512]{1,0:T(1,128)S(1)}, f32[1,512]{1,0:T(1,128)}, u32[]{:S(2)}) copy-start(f32[1,512]{1,0:T(1,128)} %param.15) | copy-start | bytes 6148
  7.2 70.5 %copy-start.3 = (f32[1,1,64,512]{3,2,1,0:T(8,128)S(1)}, f32[1,1,64,512]{3,2,1,0:T(8,128)}, u32[]{:S(2)}) copy-start(f32[1,1,64,512]{3,2,1,0:T(8,128)} %param.11) | copy-start | bytes 393220
  7.2 70.5 %copy-start.1 = (f32[1,1,512,512]{3,2,1,0:T(8,128)S(1)}, f32[1,1,512,512]{3,2,1,0:T(8,128)}, u32[]{:S(2)}) copy-start(f32[1,1,512,512]{3,2,1,0:T(8,128)} %param.9) | copy-start | bytes 3145732
  7.2 65.8 %all-gather.3.cloned.1.call-start = ((), (), s32[]{:S(2)}) async-start(), calls=%async_computation | async-start | bytes 8912896 | tf_op jit(solution)/shard_map/all_gather | solution.py:27
  79.2 9.3 %collective-permute-start = (f32[64,512]{1,0:T(8,128)S(1)}, f32[64,512]{1,0:T(8,128)S(1)}, u32[]{:S(2)}, u32[]{:S(2)}) collective-permute-start(f32[64,512]{1,0:T(8,128)S(1)} %convolution_add_fusion.4), channel_id=1, source_target_pairs={{1,0},{2,1},{3,2},{4,3},{5,4},{6,5},{7,6},{8,7},{9,8},{10,9},{11,1... | collective-permute-start | bytes 393224 | tf_op jit(solution)/shard_map/while/body/eval_jaxpr/ppermute | solution.py:15
  89.3 9.0 %collective-permute-start = (f32[64,512]{1,0:T(8,128)S(1)}, f32[64,512]{1,0:T(8,128)S(1)}, u32[]{:S(2)}, u32[]{:S(2)}) collective-permute-start(f32[64,512]{1,0:T(8,128)S(1)} %convolution_add_fusion.4), channel_id=1, source_target_pairs={{1,0},{2,1},{3,2},{4,3},{5,4},{6,5},{7,6},{8,7},{9,8},{10,9},{11,1... | collective-permute-start | bytes 393224 | tf_op jit(solution)/shard_map/while/body/eval_jaxpr/ppermute | solution.py:15
  99.1 9.0 %collective-permute-start = (f32[64,512]{1,0:T(8,128)S(1)}, f32[64,512]{1,0:T(8,128)S(1)}, u32[]{:S(2)}, u32[]{:S(2)}) collective-permute-start(f32[64,512]{1,0:T(8,128)S(1)} %convolution_add_fusion.4), channel_id=1, source_target_pairs={{1,0},{2,1},{3,2},{4,3},{5,4},{6,5},{7,6},{8,7},{9,8},{10,9},{11,1... | collective-permute-start | bytes 393224 | tf_op jit(solution)/shard_map/while/body/eval_jaxpr/ppermute | solution.py:15
  108.8 9.0 %collective-permute-start = (f32[64,512]{1,0:T(8,128)S(1)}, f32[64,512]{1,0:T(8,128)S(1)}, u32[]{:S(2)}, u32[]{:S(2)}) collective-permute-start(f32[64,512]{1,0:T(8,128)S(1)} %convolution_add_fusion.4), channel_id=1, source_target_pairs={{1,0},{2,1},{3,2},{4,3},{5,4},{6,5},{7,6},{8,7},{9,8},{10,9},{11,1... | collective-permute-start | bytes 393224 | tf_op jit(solution)/shard_map/while/body/eval_jaxpr/ppermute | solution.py:15
  118.6 9.0 %collective-permute-start = (f32[64,512]{1,0:T(8,128)S(1)}, f32[64,512]{1,0:T(8,128)S(1)}, u32[]{:S(2)}, u32[]{:S(2)}) collective-permute-start(f32[64,512]{1,0:T(8,128)S(1)} %convolution_add_fusion.4), channel_id=1, source_target_pairs={{1,0},{2,1},{3,2},{4,3},{5,4},{6,5},{7,6},{8,7},{9,8},{10,9},{11,1... | collective-permute-start | bytes 393224 | tf_op jit(solution)/shard_map/while/body/eval_jaxpr/ppermute | solution.py:15
  128.3 9.0 %collective-permute-start = (f32[64,512]{1,0:T(8,128)S(1)}, f32[64,512]{1,0:T(8,128)S(1)}, u32[]{:S(2)}, u32[]{:S(2)}) collective-permute-start(f32[64,512]{1,0:T(8,128)S(1)} %convolution_add_fusion.4), channel_id=1, source_target_pairs={{1,0},{2,1},{3,2},{4,3},{5,4},{6,5},{7,6},{8,7},{9,8},{10,9},{11,1... | collective-permute-start | bytes 393224 | tf_op jit(solution)/shard_map/while/body/eval_jaxpr/ppermute | solution.py:15
  138.1 9.1 %collective-permute-start = (f32[64,512]{1,0:T(8,128)S(1)}, f32[64,512]{1,0:T(8,128)S(1)}, u32[]{:S(2)}, u32[]{:S(2)}) collective-permute-start(f32[64,512]{1,0:T(8,128)S(1)} %convolution_add_fusion.4), channel_id=1, source_target_pairs={{1,0},{2,1},{3,2},{4,3},{5,4},{6,5},{7,6},{8,7},{9,8},{10,9},{11,1... | collective-permute-start | bytes 393224 | tf_op jit(solution)/shard_map/while/body/eval_jaxpr/ppermute | solution.py:15
  148.0 10.2 %collective-permute-start = (f32[64,512]{1,0:T(8,128)S(1)}, f32[64,512]{1,0:T(8,128)S(1)}, u32[]{:S(2)}, u32[]{:S(2)}) collective-permute-start(f32[64,512]{1,0:T(8,128)S(1)} %convolution_add_fusion.4), channel_id=1, source_target_pairs={{1,0},{2,1},{3,2},{4,3},{5,4},{6,5},{7,6},{8,7},{9,8},{10,9},{11,1... | collective-permute-start | bytes 393224 | tf_op jit(solution)/shard_map/while/body/eval_jaxpr/ppermute | solution.py:15
  159.0 9.5 %collective-permute-start = (f32[64,512]{1,0:T(8,128)S(1)}, f32[64,512]{1,0:T(8,128)S(1)}, u32[]{:S(2)}, u32[]{:S(2)}) collective-permute-start(f32[64,512]{1,0:T(8,128)S(1)} %convolution_add_fusion.4), channel_id=1, source_target_pairs={{1,0},{2,1},{3,2},{4,3},{5,4},{6,5},{7,6},{8,7},{9,8},{10,9},{11,1... | collective-permute-start | bytes 393224 | tf_op jit(solution)/shard_map/while/body/eval_jaxpr/ppermute | solution.py:15
  169.3 9.0 %collective-permute-start = (f32[64,512]{1,0:T(8,128)S(1)}, f32[64,512]{1,0:T(8,128)S(1)}, u32[]{:S(2)}, u32[]{:S(2)}) collective-permute-start(f32[64,512]{1,0:T(8,128)S(1)} %convolution_add_fusion.4), channel_id=1, source_target_pairs={{1,0},{2,1},{3,2},{4,3},{5,4},{6,5},{7,6},{8,7},{9,8},{10,9},{11,1... | collective-permute-start | bytes 393224 | tf_op jit(solution)/shard_map/while/body/eval_jaxpr/ppermute | solution.py:15
  179.1 9.0 %collective-permute-start = (f32[64,512]{1,0:T(8,128)S(1)}, f32[64,512]{1,0:T(8,128)S(1)}, u32[]{:S(2)}, u32[]{:S(2)}) collective-permute-start(f32[64,512]{1,0:T(8,128)S(1)} %convolution_add_fusion.4), channel_id=1, source_target_pairs={{1,0},{2,1},{3,2},{4,3},{5,4},{6,5},{7,6},{8,7},{9,8},{10,9},{11,1... | collective-permute-start | bytes 393224 | tf_op jit(solution)/shard_map/while/body/eval_jaxpr/ppermute | solution.py:15
  188.9 9.0 %collective-permute-start = (f32[64,512]{1,0:T(8,128)S(1)}, f32[64,512]{1,0:T(8,128)S(1)}, u32[]{:S(2)}, u32[]{:S(2)}) collective-permute-start(f32[64,512]{1,0:T(8,128)S(1)} %convolution_add_fusion.4), channel_id=1, source_target_pairs={{1,0},{2,1},{3,2},{4,3},{5,4},{6,5},{7,6},{8,7},{9,8},{10,9},{11,1... | collective-permute-start | bytes 393224 | tf_op jit(solution)/shard_map/while/body/eval_jaxpr/ppermute | solution.py:15
  198.6 9.0 %collective-permute-start = (f32[64,512]{1,0:T(8,128)S(1)}, f32[64,512]{1,0:T(8,128)S(1)}, u32[]{:S(2)}, u32[]{:S(2)}) collective-permute-start(f32[64,512]{1,0:T(8,128)S(1)} %convolution_add_fusion.4), channel_id=1, source_target_pairs={{1,0},{2,1},{3,2},{4,3},{5,4},{6,5},{7,6},{8,7},{9,8},{10,9},{11,1... | collective-permute-start | bytes 393224 | tf_op jit(solution)/shard_map/while/body/eval_jaxpr/ppermute | solution.py:15
  208.4 9.0 %collective-permute-start = (f32[64,512]{1,0:T(8,128)S(1)}, f32[64,512]{1,0:T(8,128)S(1)}, u32[]{:S(2)}, u32[]{:S(2)}) collective-permute-start(f32[64,512]{1,0:T(8,128)S(1)} %convolution_add_fusion.4), channel_id=1, source_target_pairs={{1,0},{2,1},{3,2},{4,3},{5,4},{6,5},{7,6},{8,7},{9,8},{10,9},{11,1... | collective-permute-start | bytes 393224 | tf_op jit(solution)/shard_map/while/body/eval_jaxpr/ppermute | solution.py:15
  218.1 9.2 %collective-permute-start = (f32[64,512]{1,0:T(8,128)S(1)}, f32[64,512]{1,0:T(8,128)S(1)}, u32[]{:S(2)}, u32[]{:S(2)}) collective-permute-start(f32[64,512]{1,0:T(8,128)S(1)} %convolution_add_fusion.4), channel_id=1, source_target_pairs={{1,0},{2,1},{3,2},{4,3},{5,4},{6,5},{7,6},{8,7},{9,8},{10,9},{11,1... | collective-permute-start | bytes 393224 | tf_op jit(solution)/shard_map/while/body/eval_jaxpr/ppermute | solution.py:15
  228.1 10.4 %collective-permute-start = (f32[64,512]{1,0:T(8,128)S(1)}, f32[64,512]{1,0:T(8,128)S(1)}, u32[]{:S(2)}, u32[]{:S(2)}) collective-permute-start(f32[64,512]{1,0:T(8,128)S(1)} %convolution_add_fusion.4), channel_id=1, source_target_pairs={{1,0},{2,1},{3,2},{4,3},{5,4},{6,5},{7,6},{8,7},{9,8},{10,9},{11,1... | collective-permute-start | bytes 393224 | tf_op jit(solution)/shard_map/while/body/eval_jaxpr/ppermute | solution.py:15
  239.3 9.5 %collective-permute-start = (f32[64,512]{1,0:T(8,128)S(1)}, f32[64,512]{1,0:T(8,128)S(1)}, u32[]{:S(2)}, u32[]{:S(2)}) collective-permute-start(f32[64,512]{1,0:T(8,128)S(1)} %convolution_add_fusion.4), channel_id=1, source_target_pairs={{1,0},{2,1},{3,2},{4,3},{5,4},{6,5},{7,6},{8,7},{9,8},{10,9},{11,1... | collective-permute-start | bytes 393224 | tf_op jit(solution)/shard_map/while/body/eval_jaxpr/ppermute | solution.py:15
  249.6 9.0 %collective-permute-start = (f32[64,512]{1,0:T(8,128)S(1)}, f32[64,512]{1,0:T(8,128)S(1)}, u32[]{:S(2)}, u32[]{:S(2)}) collective-permute-start(f32[64,512]{1,0:T(8,128)S(1)} %convolution_add_fusion.4), channel_id=1, source_target_pairs={{1,0},{2,1},{3,2},{4,3},{5,4},{6,5},{7,6},{8,7},{9,8},{10,9},{11,1... | collective-permute-start | bytes 393224 | tf_op jit(solution)/shard_map/while/body/eval_jaxpr/ppermute | solution.py:15
  259.4 9.0 %collective-permute-start = (f32[64,512]{1,0:T(8,128)S(1)}, f32[64,512]{1,0:T(8,128)S(1)}, u32[]{:S(2)}, u32[]{:S(2)}) collective-permute-start(f32[64,512]{1,0:T(8,128)S(1)} %convolution_add_fusion.4), channel_id=1, source_target_pairs={{1,0},{2,1},{3,2},{4,3},{5,4},{6,5},{7,6},{8,7},{9,8},{10,9},{11,1... | collective-permute-start | bytes 393224 | tf_op jit(solution)/shard_map/while/body/eval_jaxpr/ppermute | solution.py:15
  269.1 9.0 %collective-permute-start = (f32[64,512]{1,0:T(8,128)S(1)}, f32[64,512]{1,0:T(8,128)S(1)}, u32[]{:S(2)}, u32[]{:S(2)}) collective-permute-start(f32[64,512]{1,0:T(8,128)S(1)} %convolution_add_fusion.4), channel_id=1, source_target_pairs={{1,0},{2,1},{3,2},{4,3},{5,4},{6,5},{7,6},{8,7},{9,8},{10,9},{11,1... | collective-permute-start | bytes 393224 | tf_op jit(solution)/shard_map/while/body/eval_jaxpr/ppermute | solution.py:15
  278.9 9.0 %collective-permute-start = (f32[64,512]{1,0:T(8,128)S(1)}, f32[64,512]{1,0:T(8,128)S(1)}, u32[]{:S(2)}, u32[]{:S(2)}) collective-permute-start(f32[64,512]{1,0:T(8,128)S(1)} %convolution_add_fusion.4), channel_id=1, source_target_pairs={{1,0},{2,1},{3,2},{4,3},{5,4},{6,5},{7,6},{8,7},{9,8},{10,9},{11,1... | collective-permute-start | bytes 393224 | tf_op jit(solution)/shard_map/while/body/eval_jaxpr/ppermute | solution.py:15
  288.6 9.0 %collective-permute-start = (f32[64,512]{1,0:T(8,128)S(1)}, f32[64,512]{1,0:T(8,128)S(1)}, u32[]{:S(2)}, u32[]{:S(2)}) collective-permute-start(f32[64,512]{1,0:T(8,128)S(1)} %convolution_add_fusion.4), channel_id=1, source_target_pairs={{1,0},{2,1},{3,2},{4,3},{5,4},{6,5},{7,6},{8,7},{9,8},{10,9},{11,1... | collective-permute-start | bytes 393224 | tf_op jit(solution)/shard_map/while/body/eval_jaxpr/ppermute | solution.py:15
  298.4 9.2 %collective-permute-start = (f32[64,512]{1,0:T(8,128)S(1)}, f32[64,512]{1,0:T(8,128)S(1)}, u32[]{:S(2)}, u32[]{:S(2)}) collective-permute-start(f32[64,512]{1,0:T(8,128)S(1)} %convolution_add_fusion.4), channel_id=1, source_target_pairs={{1,0},{2,1},{3,2},{4,3},{5,4},{6,5},{7,6},{8,7},{9,8},{10,9},{11,1... | collective-permute-start | bytes 393224 | tf_op jit(solution)/shard_map/while/body/eval_jaxpr/ppermute | solution.py:15
  308.4 10.4 %collective-permute-start = (f32[64,512]{1,0:T(8,128)S(1)}, f32[64,512]{1,0:T(8,128)S(1)}, u32[]{:S(2)}, u32[]{:S(2)}) collective-permute-start(f32[64,512]{1,0:T(8,128)S(1)} %convolution_add_fusion.4), channel_id=1, source_target_pairs={{1,0},{2,1},{3,2},{4,3},{5,4},{6,5},{7,6},{8,7},{9,8},{10,9},{11,1... | collective-permute-start | bytes 393224 | tf_op jit(solution)/shard_map/while/body/eval_jaxpr/ppermute | solution.py:15
  319.5 9.5 %collective-permute-start = (f32[64,512]{1,0:T(8,128)S(1)}, f32[64,512]{1,0:T(8,128)S(1)}, u32[]{:S(2)}, u32[]{:S(2)}) collective-permute-start(f32[64,512]{1,0:T(8,128)S(1)} %convolution_add_fusion.4), channel_id=1, source_target_pairs={{1,0},{2,1},{3,2},{4,3},{5,4},{6,5},{7,6},{8,7},{9,8},{10,9},{11,1... | collective-permute-start | bytes 393224 | tf_op jit(solution)/shard_map/while/body/eval_jaxpr/ppermute | solution.py:15
  329.8 9.0 %collective-permute-start = (f32[64,512]{1,0:T(8,128)S(1)}, f32[64,512]{1,0:T(8,128)S(1)}, u32[]{:S(2)}, u32[]{:S(2)}) collective-permute-start(f32[64,512]{1,0:T(8,128)S(1)} %convolution_add_fusion.4), channel_id=1, source_target_pairs={{1,0},{2,1},{3,2},{4,3},{5,4},{6,5},{7,6},{8,7},{9,8},{10,9},{11,1... | collective-permute-start | bytes 393224 | tf_op jit(solution)/shard_map/while/body/eval_jaxpr/ppermute | solution.py:15
  339.6 9.0 %collective-permute-start = (f32[64,512]{1,0:T(8,128)S(1)}, f32[64,512]{1,0:T(8,128)S(1)}, u32[]{:S(2)}, u32[]{:S(2)}) collective-permute-start(f32[64,512]{1,0:T(8,128)S(1)} %convolution_add_fusion.4), channel_id=1, source_target_pairs={{1,0},{2,1},{3,2},{4,3},{5,4},{6,5},{7,6},{8,7},{9,8},{10,9},{11,1... | collective-permute-start | bytes 393224 | tf_op jit(solution)/shard_map/while/body/eval_jaxpr/ppermute | solution.py:15
  349.4 9.0 %collective-permute-start = (f32[64,512]{1,0:T(8,128)S(1)}, f32[64,512]{1,0:T(8,128)S(1)}, u32[]{:S(2)}, u32[]{:S(2)}) collective-permute-start(f32[64,512]{1,0:T(8,128)S(1)} %convolution_add_fusion.4), channel_id=1, source_target_pairs={{1,0},{2,1},{3,2},{4,3},{5,4},{6,5},{7,6},{8,7},{9,8},{10,9},{11,1... | collective-permute-start | bytes 393224 | tf_op jit(solution)/shard_map/while/body/eval_jaxpr/ppermute | solution.py:15
  359.1 9.0 %collective-permute-start = (f32[64,512]{1,0:T(8,128)S(1)}, f32[64,512]{1,0:T(8,128)S(1)}, u32[]{:S(2)}, u32[]{:S(2)}) collective-permute-start(f32[64,512]{1,0:T(8,128)S(1)} %convolution_add_fusion.4), channel_id=1, source_target_pairs={{1,0},{2,1},{3,2},{4,3},{5,4},{6,5},{7,6},{8,7},{9,8},{10,9},{11,1... | collective-permute-start | bytes 393224 | tf_op jit(solution)/shard_map/while/body/eval_jaxpr/ppermute | solution.py:15
  368.9 9.0 %collective-permute-start = (f32[64,512]{1,0:T(8,128)S(1)}, f32[64,512]{1,0:T(8,128)S(1)}, u32[]{:S(2)}, u32[]{:S(2)}) collective-permute-start(f32[64,512]{1,0:T(8,128)S(1)} %convolution_add_fusion.4), channel_id=1, source_target_pairs={{1,0},{2,1},{3,2},{4,3},{5,4},{6,5},{7,6},{8,7},{9,8},{10,9},{11,1... | collective-permute-start | bytes 393224 | tf_op jit(solution)/shard_map/while/body/eval_jaxpr/ppermute | solution.py:15
  378.6 9.0 %collective-permute-start = (f32[64,512]{1,0:T(8,128)S(1)}, f32[64,512]{1,0:T(8,128)S(1)}, u32[]{:S(2)}, u32[]{:S(2)}) collective-permute-start(f32[64,512]{1,0:T(8,128)S(1)} %convolution_add_fusion.4), channel_id=1, source_target_pairs={{1,0},{2,1},{3,2},{4,3},{5,4},{6,5},{7,6},{8,7},{9,8},{10,9},{11,1... | collective-permute-start | bytes 393224 | tf_op jit(solution)/shard_map/while/body/eval_jaxpr/ppermute | solution.py:15
Sparse Core Ops, SparseCore 0:
  10.7 62.2 all-gather.2
